TPU v7x, 32 devices: a whole 2x2x4 slice. The times are simulated.
32 devices in a mesh: dp: 8 (over z, y), tensor: 4 (over x, core).
Axes of the slice: x: 2, y: 2, z: 4, core: 2. Of those that a mesh axis runs over, the one named last changes fastest.
Arguments:
- tokens: bfloat16 [8192, 2048], P('dp'), may hold values from -6 to 6
- segment_ids: int32 [8, 1024], P('dp'), may hold values from 0 to 7, never falling along the last dimension, each value on 1 to 512 neighbouring positions
- attn_gain: bfloat16 [2048], P('dp'), may hold values from 0.25 to 1.75
- query_weight: bfloat16 [2048, 2048], P('dp', 'tensor'), may hold values from -0.125 to 0.125
- key_weight: bfloat16 [2048, 512], P('dp', 'tensor'), may hold values from -0.125 to 0.125
- value_weight: bfloat16 [2048, 512], P('dp', 'tensor'), may hold values from -0.125 to 0.125
- output_weight: bfloat16 [2048, 2048], P('tensor', 'dp'), may hold values from -0.5 to 0.5
- ffn_gain: bfloat16 [2048], P('dp'), may hold values from 0.25 to 1.75
- gate_weight: bfloat16 [2048, 8192], P('dp', 'tensor'), may hold values from -0.125 to 0.125
- up_weight: bfloat16 [2048, 8192], P('dp', 'tensor'), may hold values from -0.125 to 0.125
- down_weight: bfloat16 [8192, 2048], P('tensor', 'dp'), may hold values from -0.0625 to 0.0625
- cotangent: bfloat16 [8192, 2048], P('dp'), may hold values from -6 to 6
Outputs:
- layer_output: bfloat16 [8192, 2048], P('dp')
- tokens_grad: float32 [8192, 2048], P('dp')
- attn_gain_grad: float32 [2048], P('dp')
- query_weight_grad: float32 [2048, 2048], P('dp', 'tensor')
- key_weight_grad: float32 [2048, 512], P('dp', 'tensor')
- value_weight_grad: float32 [2048, 512], P('dp', 'tensor')
- output_weight_grad: float32 [2048, 2048], P('tensor', 'dp')
- ffn_gain_grad: float32 [2048], P('dp')
- gate_weight_grad: float32 [2048, 8192], P('dp', 'tensor')
- up_weight_grad: float32 [2048, 8192], P('dp', 'tensor')
- down_weight_grad: float32 [8192, 2048], P('tensor', 'dp')
Inputs may be any that keep to these rules, and one draw needn't show every extreme that they name: In each row of segment_ids the numbers never fall; each document spans 1 to 512 positions, and one spans exactly 512.
All inputs are finite; a program needn't handle non-finite values.
Results may differ from a plain program's by a relative error of at most 0.02.
Values may be sent and summed in bfloat16 or wider, within the bound.
A program may use at most 256 MiB of HBM per device.

v0:
```python
from functools import partial
import math
import jax
import jax.numpy as jnp
from jax import lax
from jax.sharding import PartitionSpec as P

HD = 64
epsilon = 1e-05


def rope_tables(segment_row, head_size):
    length = segment_row.shape[0]
    places = jnp.arange(length, dtype=jnp.int32)
    boundary = jnp.concatenate([jnp.ones((1,), dtype=bool), segment_row[1:] != segment_row[:-1]])
    starts = lax.cummax(jnp.where(boundary, places, 0), axis=0)
    position = (places - starts).astype(jnp.float32)
    half_size = head_size // 2
    exponent = jnp.arange(half_size, dtype=jnp.float32) * 2.0 / head_size
    inverse = 1.0 / 500000.0**exponent
    wavelen = 2.0 * math.pi / inverse
    smooth = (8192.0 / wavelen - 1.0) / 3.0
    scaled = jnp.where(
        wavelen < 2048.0,
        inverse,
        jnp.where(
            wavelen > 8192.0, inverse / 32.0, (1.0 - smooth) * inverse / 32.0 + smooth * inverse
        ),
    )
    angles = position[:, None] * scaled[None, :]
    cosine_table = jnp.cos(angles)
    sine_table = jnp.sin(angles)
    return (
        jnp.concatenate([cosine_table, cosine_table], axis=-1),
        jnp.concatenate([sine_table, sine_table], axis=-1),
    )


def rotate(values, cosine_table, sine_table):
    half_size = values.shape[-1] // 2
    turned = jnp.concatenate([-values[..., half_size:], values[..., :half_size]], axis=-1)
    return values * cosine_table + turned * sine_table


def rms_norm(values, gain_vector):
    factor = lax.rsqrt(jnp.mean(values * values, axis=-1, keepdims=True) + epsilon)
    return values * factor * gain_vector


def swiglu(gate_values, up_values):
    return jax.nn.silu(gate_values) * up_values


def contract_rows(left_side, right_side):
    return lax.dot_general(
        left_side, right_side, (((0,), (0,)), ((), ())), preferred_element_type=jnp.float32
    )


def contract_cols(left_side, right_side):
    return lax.dot_general(
        left_side, right_side, (((1,), (1,)), ((), ())), preferred_element_type=jnp.float32
    )


def block_scores(query_block, key_seq, segment_row, start_row):
    row_count = query_block.shape[0]
    length = key_seq.shape[0]
    score_scale = query_block.shape[-1] ** (-0.5)
    scores = (
        jnp.einsum("qkgd,skd->kgqs", query_block, key_seq, preferred_element_type=jnp.float32)
        * score_scale
    )
    row_ids = start_row + jnp.arange(row_count, dtype=jnp.int32)
    col_ids = jnp.arange(length, dtype=jnp.int32)
    same_doc = segment_row[start_row : start_row + row_count][:, None] == segment_row[None, :]
    allowed = same_doc & (col_ids[None, :] <= row_ids[:, None])
    return jnp.where(allowed, scores, -1000000000.0)


def attend_forward(operands):
    query_seq, key_seq, value_seq, segment_row = operands
    length, kv_local, head_size = key_seq.shape
    grouped = query_seq.reshape(length, kv_local, -1, head_size)
    block_rows = min(512, length)
    mixed_parts = []
    total_parts = []
    for start_row in range(0, length, block_rows):
        scores = block_scores(
            grouped[start_row : start_row + block_rows], key_seq, segment_row, start_row
        )
        row_max = jnp.max(scores, axis=-1, keepdims=True)
        log_total = jnp.log(jnp.sum(jnp.exp(scores - row_max), axis=-1, keepdims=True)) + row_max
        soft_low = jnp.exp(scores - log_total).astype(jnp.bfloat16)
        mixed_block = jnp.einsum(
            "kgqs,skd->qkgd", soft_low, value_seq, preferred_element_type=jnp.float32
        )
        mixed_parts.append(mixed_block.reshape(block_rows, -1).astype(jnp.bfloat16))
        total_parts.append(log_total)
    return (jnp.concatenate(mixed_parts, axis=0), jnp.concatenate(total_parts, axis=2))


def attend_backward(operands):
    query_seq, key_seq, value_seq, log_total, grad_seq, segment_row = operands
    length, kv_local, head_size = key_seq.shape
    grouped = query_seq.reshape(length, kv_local, -1, head_size)
    grad_grouped = grad_seq.reshape(length, kv_local, -1, head_size)
    block_rows = min(512, length)
    score_scale = head_size ** (-0.5)
    query_parts = []
    key_grad = jnp.zeros(key_seq.shape, jnp.float32)
    value_grad = jnp.zeros(value_seq.shape, jnp.float32)
    for start_row in range(0, length, block_rows):
        query_block = grouped[start_row : start_row + block_rows]
        grad_block = grad_grouped[start_row : start_row + block_rows]
        scores = block_scores(query_block, key_seq, segment_row, start_row)
        soft_weights = jnp.exp(scores - log_total[:, :, start_row : start_row + block_rows])
        soft_grad = jnp.einsum(
            "qkgd,skd->kgqs", grad_block, value_seq, preferred_element_type=jnp.float32
        )
        score_grad = (
            soft_weights * (soft_grad - jnp.sum(soft_weights * soft_grad, axis=-1, keepdims=True))
        ).astype(jnp.bfloat16)
        query_parts.append(
            jnp.einsum("kgqs,skd->qkgd", score_grad, key_seq, preferred_element_type=jnp.float32)
            * score_scale
        )
        key_grad = (
            key_grad
            + jnp.einsum(
                "kgqs,qkgd->skd", score_grad, query_block, preferred_element_type=jnp.float32
            )
            * score_scale
        )
        value_grad = value_grad + jnp.einsum(
            "kgqs,qkgd->skd",
            soft_weights.astype(jnp.bfloat16),
            grad_block,
            preferred_element_type=jnp.float32,
        )
    query_grad = jnp.concatenate(query_parts, axis=0).reshape(length, -1, head_size)
    return (query_grad, key_grad, value_grad)


def shards(
    tokens,
    segment_ids,
    attn_gain,
    query_weight,
    key_weight,
    value_weight,
    output_weight,
    ffn_gain,
    gate_weight,
    up_weight,
    down_weight,
    cotangent,
):
    gathered = (
        lax.all_gather(attn_gain, "dp", axis=0, tiled=True),
        lax.all_gather(query_weight, "dp", axis=0, tiled=True),
        lax.all_gather(key_weight, "dp", axis=0, tiled=True),
        lax.all_gather(value_weight, "dp", axis=0, tiled=True),
        lax.all_gather(output_weight, "dp", axis=1, tiled=True),
        lax.all_gather(ffn_gain, "dp", axis=0, tiled=True),
        lax.all_gather(gate_weight, "dp", axis=0, tiled=True),
        lax.all_gather(up_weight, "dp", axis=0, tiled=True),
        lax.all_gather(down_weight, "dp", axis=1, tiled=True),
    )
    seq_count, length = segment_ids.shape
    token_count = tokens.shape[0]
    tokens_float = tokens.astype(jnp.float32)
    cotangent_float = cotangent.astype(jnp.float32)
    attn_scale = gathered[0].astype(jnp.float32)
    ffn_scale = gathered[5].astype(jnp.float32)
    normed = rms_norm(tokens_float, attn_scale).astype(jnp.bfloat16)
    query_raw = jnp.dot(normed, gathered[1], preferred_element_type=jnp.float32)
    key_raw = jnp.dot(normed, gathered[2], preferred_element_type=jnp.float32)
    value_low = jnp.dot(normed, gathered[3], preferred_element_type=jnp.float32).astype(
        jnp.bfloat16
    )
    cosine_table, sine_table = jax.vmap(partial(rope_tables, head_size=HD))(segment_ids)
    cosine_wide = cosine_table[:, :, None, :]
    sine_wide = sine_table[:, :, None, :]
    query_shaped = query_raw.reshape(seq_count, length, -1, HD)
    key_shaped = key_raw.reshape(seq_count, length, -1, HD)
    query_low = rotate(query_shaped, cosine_wide, sine_wide).astype(jnp.bfloat16)
    key_low = rotate(key_shaped, cosine_wide, sine_wide).astype(jnp.bfloat16)
    value_seqs = value_low.reshape(seq_count, length, -1, HD)
    mixed_low, log_total = lax.map(attend_forward, (query_low, key_low, value_seqs, segment_ids))
    mixed_low = mixed_low.reshape(token_count, -1)
    attn_part = jnp.dot(mixed_low, gathered[4], preferred_element_type=jnp.float32)
    hidden_state = tokens_float + lax.psum(attn_part, "tensor")
    normed_two = rms_norm(hidden_state, ffn_scale).astype(jnp.bfloat16)
    gate_values = jnp.dot(normed_two, gathered[6], preferred_element_type=jnp.float32)
    up_values = jnp.dot(normed_two, gathered[7], preferred_element_type=jnp.float32)
    active = swiglu(gate_values, up_values).astype(jnp.bfloat16)
    ffn_part = jnp.dot(active, gathered[8], preferred_element_type=jnp.float32)
    layer_output = (
        hidden_state + lax.psum(ffn_part.astype(jnp.bfloat16), "tensor").astype(jnp.float32)
    ).astype(jnp.bfloat16)
    down_grad = contract_rows(active, cotangent)
    active_grad = contract_cols(cotangent, gathered[8])
    unused_value, swiglu_pull = jax.vjp(swiglu, gate_values, up_values)
    gate_grad, up_grad = swiglu_pull(active_grad)
    gate_low = gate_grad.astype(jnp.bfloat16)
    up_low = up_grad.astype(jnp.bfloat16)
    gate_weight_grad = contract_rows(normed_two, gate_low)
    up_weight_grad = contract_rows(normed_two, up_low)
    mlp_part = contract_cols(gate_low, gathered[6]) + contract_cols(up_low, gathered[7])
    normed_two_grad = lax.psum(mlp_part, "tensor")
    unused_second, second_pull = jax.vjp(rms_norm, hidden_state, ffn_scale)
    hidden_part, ffn_gain_grad = second_pull(normed_two_grad)
    hidden_grad = cotangent_float + hidden_part
    hidden_low = hidden_grad.astype(jnp.bfloat16)
    output_weight_grad = contract_rows(mixed_low, hidden_low)
    mixed_grad = contract_cols(hidden_low, gathered[4]).astype(jnp.bfloat16)
    query_grad, key_grad, value_grad = lax.map(
        attend_backward,
        (
            query_low,
            key_low,
            value_seqs,
            log_total,
            mixed_grad.reshape(seq_count, length, -1, HD),
            segment_ids,
        ),
    )
    unused_query, query_pull = jax.vjp(
        partial(rotate, cosine_table=cosine_wide, sine_table=sine_wide), query_shaped
    )
    unused_key, key_pull = jax.vjp(
        partial(rotate, cosine_table=cosine_wide, sine_table=sine_wide), key_shaped
    )
    query_raw_grad = query_pull(query_grad)[0].reshape(token_count, -1).astype(jnp.bfloat16)
    key_raw_grad = key_pull(key_grad)[0].reshape(token_count, -1).astype(jnp.bfloat16)
    value_raw_grad = value_grad.reshape(token_count, -1).astype(jnp.bfloat16)
    query_weight_grad = contract_rows(normed, query_raw_grad)
    key_weight_grad = contract_rows(normed, key_raw_grad)
    value_weight_grad = contract_rows(normed, value_raw_grad)
    attn_back_part = (
        contract_cols(query_raw_grad, gathered[1])
        + contract_cols(key_raw_grad, gathered[2])
        + contract_cols(value_raw_grad, gathered[3])
    )
    normed_grad = lax.psum(attn_back_part.astype(jnp.bfloat16), "tensor").astype(jnp.float32)
    unused_first, first_pull = jax.vjp(rms_norm, tokens_float, attn_scale)
    token_part, attn_gain_grad = first_pull(normed_grad)
    tokens_grad = hidden_grad + token_part
    summed = (
        lax.psum_scatter(
            attn_gain_grad.astype(jnp.bfloat16), "dp", scatter_dimension=0, tiled=True
        ).astype(jnp.float32),
        lax.psum_scatter(
            query_weight_grad.astype(jnp.bfloat16), "dp", scatter_dimension=0, tiled=True
        ).astype(jnp.float32),
        lax.psum_scatter(
            key_weight_grad.astype(jnp.bfloat16), "dp", scatter_dimension=0, tiled=True
        ).astype(jnp.float32),
        lax.psum_scatter(
            value_weight_grad.astype(jnp.bfloat16), "dp", scatter_dimension=0, tiled=True
        ).astype(jnp.float32),
        lax.psum_scatter(
            output_weight_grad.astype(jnp.bfloat16), "dp", scatter_dimension=1, tiled=True
        ).astype(jnp.float32),
        lax.psum_scatter(
            ffn_gain_grad.astype(jnp.bfloat16), "dp", scatter_dimension=0, tiled=True
        ).astype(jnp.float32),
        lax.psum_scatter(
            gate_weight_grad.astype(jnp.bfloat16), "dp", scatter_dimension=0, tiled=True
        ).astype(jnp.float32),
        lax.psum_scatter(
            up_weight_grad.astype(jnp.bfloat16), "dp", scatter_dimension=0, tiled=True
        ).astype(jnp.float32),
        lax.psum_scatter(
            down_grad.astype(jnp.bfloat16), "dp", scatter_dimension=1, tiled=True
        ).astype(jnp.float32),
    )
    attn_gain_total = summed[0]
    ffn_gain_total = summed[5]
    return (
        layer_output,
        tokens_grad,
        attn_gain_total,
        summed[1],
        summed[2],
        summed[3],
        summed[4],
        ffn_gain_total,
        summed[6],
        summed[7],
        summed[8],
    )


def solution(mesh):
    return jax.shard_map(
        shards,
        mesh=mesh,
        in_specs=(
            P("dp", None),
            P("dp", None),
            P("dp"),
            P("dp", "tensor"),
            P("dp", "tensor"),
            P("dp", "tensor"),
            P("tensor", "dp"),
            P("dp"),
            P("dp", "tensor"),
            P("dp", "tensor"),
            P("tensor", "dp"),
            P("dp", None),
        ),
        out_specs=(
            P("dp", None),
            P("dp", None),
            P("dp"),
            P("dp", "tensor"),
            P("dp", "tensor"),
            P("dp", "tensor"),
            P("tensor", "dp"),
            P("dp"),
            P("dp", "tensor"),
            P("dp", "tensor"),
            P("tensor", "dp"),
        ),
        check_vma=False,
    )
```

profile of v0, /device:TPU:0, one launch (start us, length us, event | category | flops | bytes accessed | tf_op | source)
XLA Modules:
  0.0 1853.7 jit_solution(15969643140244901022)
XLA Ops:
  15.5 22.5 %all-gather = bf16[8,1,256]{2,1,0:T(2,128)(2,1)S(1)} all-gather(bf16[1,1,256]{2,1,0:T(2,128)(2,1)S(1)} %reshape.443), channel_id=1, replica_groups=mesh['dp'=8,'tensor'=4] {'dp'}, dimensions={0}, use_global_device_ids=true | all-gather | bytes 4608 | tf_op jit(solution)/shard_map/all_gather | solution.py:160
  38.7 33.1 %all_gather.29 = bf16[2048,128]{1,0:T(8,128)(2,1)S(1)} all-gather(bf16[256,128]{1,0:T(8,128)(2,1)} %param.16), channel_id=1, replica_groups=mesh['dp'=8,'tensor'=4] {'dp'}, dimensions={0}, use_global_device_ids=true | all-gather | bytes 589824 | tf_op jit(solution)/shard_map/all_gather | solution.py:162
  71.8 32.3 %all_gather.28 = bf16[2048,128]{1,0:T(8,128)(2,1)S(1)} all-gather(bf16[256,128]{1,0:T(8,128)(2,1)} %param.17), channel_id=1, replica_groups=mesh['dp'=8,'tensor'=4] {'dp'}, dimensions={0}, use_global_device_ids=true | all-gather | bytes 589824 | tf_op jit(solution)/shard_map/all_gather | solution.py:163
  112.1 5.3 fusion.64
  118.3 7.7 fusion.11
  126.0 9.2 exponential_reduce_fusion
  135.3 7.3 fusion.10
  142.6 9.2 exponential_reduce_fusion.1
  151.8 8.4 convolution_convert_fusion.8
  166.7 7.5 fusion.41
  176.0 16.3 all-gather.1
  192.3 132.1 %all-reduce.12.cloned.1.call-done = f32[1024,2048]{1,0:T(8,128)} async-done(((f32[1024,2048]{1,0:T(8,128)}), f32[1024,2048]{1,0:T(8,128)}) %all-reduce.12.cloned.1.call-update) | async-done | bytes 8388624 | tf_op jit(solution)/shard_map/psum | solution.py:193
  324.5 5.7 multiply_reduce_fusion.2
  336.3 114.8 %all-gather.14.cloned.1.call-done = bf16[2048,2048]{1,0:T(8,128)(2,1)} async-done(((bf16[256,2048]{1,0:T(8,128)(2,1)}), bf16[2048,2048]{1,0:T(8,128)(2,1)}) %all-gather.14.cloned.1.call-update) | async-done | bytes 8388624 | tf_op jit(solution)/shard_map/all_gather | solution.py:167
  451.1 14.7 fusion.66
  465.8 110.0 %all-gather.12.cloned.1.call-done = bf16[2048,2048]{1,0:T(8,128)(2,1)} async-done(((bf16[256,2048]{1,0:T(8,128)(2,1)}), bf16[2048,2048]{1,0:T(8,128)(2,1)}) %all-gather.12.cloned.1.call-update) | async-done | bytes 8388624 | tf_op jit(solution)/shard_map/all_gather | solution.py:166
  575.8 14.6 fusion.65
  590.3 110.5 %all-gather.16.cloned.1.call-done = bf16[2048,2048]{1,0:T(8,128)(2,1)} async-done(((bf16[2048,256]{1,0:T(8,128)(2,1)}), bf16[2048,2048]{1,0:T(8,128)(2,1)}) %all-gather.16.cloned.1.call-update) | async-done | bytes 8388624 | tf_op jit(solution)/shard_map/all_gather | solution.py:168
  700.8 21.7 %multiply_convert_fusion = (bf16[1024,2048]{1,0:T(8,128)(2,1)}, bf16[1024,2048]{1,0:T(8,128)(2,1)}, bf16[1024,2048]{1,0:T(8,128)(2,1)}) fusion(f32[1024,2048]{1,0:T(8,128)} %fusion.65, f32[1024,2048]{1,0:T(8,128)} %fusion.66, bf16[1024,2048]{1,0:T(8,128)(2,1)} %param.23, bf16[2048,2048]{1,0:T(8,128)(2,1)} %all-gather.16.cloned.1.call-done), kind=kOutput, calls=%fused_computation.44 | convolution fusion | flops 8623489024 | bytes 41943040 | tf_op jit(solution)/shard_map/dot_general | solution.py:61
  722.5 13.1 fusion.67
  735.7 13.6 convolution_add_fusion
  751.1 149.5 %all-reduce.14.cloned.1.call-done = f32[1024,2048]{1,0:T(8,128)} async-done(((f32[1024,2048]{1,0:T(8,128)}), f32[1024,2048]{1,0:T(8,128)}) %all-reduce.14.cloned.1.call-update) | async-done | bytes 8388624 | tf_op jit(solution)/shard_map/psum | solution.py:211
  900.6 7.9 multiply_reduce_fusion
  908.5 9.6 fusion.17
  918.1 6.6 fusion.32
  925.4 5.2 convolution_bitcast_fusion
  930.6 9.4 fusion
  940.0 13.8 fusion.3
  953.8 8.6 fusion.40
  964.7 30.0 %fusion.2 = (bf16[2,4,512,1024]{2,3,1,0:T(8,128)(2,1)}, bf16[2,4,512,1024]{2,3,1,0:T(8,128)(2,1)}) fusion(f32[2,1024,512,4]{2,1,3,0:T(8,128)} %get-tuple-element.98, f32[2,1024,512,4]{2,1,3,0:T(8,128)} %get-tuple-element.94, f32[2,4,512]{2,1,0:T(4,128)S(1)} %copy-done.35, f32[2,4,512]{2,1,0:T(4,128)S(1)} %bitcast.237, ...), kind=kLoop, calls=%fused_computation.4 | loop fusion | flops 50331648 | bytes 85000192 | tf_op jit(solution)/shard_map/while/body/eval_jaxpr/convert_element_type | solution.py:123
  994.7 6.2 convolution_bitcast_fusion.2
  1006.0 7.1 convolution_convert_fusion.4
  1013.4 5.0 fusion.35
  1018.4 5.0 fusion.36
  1029.6 13.8 convolution_convert_fusion.3
  1051.0 14.1 convolution_convert_fusion
  1065.2 14.1 convolution_convert_fusion.1
  1079.6 14.2 convolution_convert_fusion.2
  1098.7 66.6 %reduce-scatter.14.cloned.1.call-done = bf16[512,256]{1,0:T(8,128)(2,1)} async-done(((bf16[512,2048]{1,0:T(8,128)(2,1)}), bf16[512,256]{1,0:T(8,128)(2,1)}) %reduce-scatter.14.cloned.1.call-update) | async-done | bytes 262160 | tf_op jit(solution)/shard_map/reduce_scatter | solution.py:263
  1167.0 69.8 %reduce-scatter.8.cloned.1.call-done = bf16[256,512]{1,0:T(8,128)(2,1)} async-done(((bf16[2048,512]{1,0:T(8,128)(2,1)}), bf16[256,512]{1,0:T(8,128)(2,1)}) %reduce-scatter.8.cloned.1.call-update) | async-done | bytes 262160 | tf_op jit(solution)/shard_map/reduce_scatter | solution.py:254
  1238.6 153.1 %all-reduce.16.cloned.1.call-done = (bf16[1024,2048]{1,0:T(8,128)(2,1)}, bf16[1024,2048]{1,0:T(8,128)(2,1)}) async-done(((bf16[1024,2048]{1,0:T(8,128)(2,1)}, bf16[1024,2048]{1,0:T(8,128)(2,1)}), (bf16[1024,2048]{1,0:T(8,128)(2,1)}, bf16[1024,2048]{1,0:T(8,128)(2,1)})) %all-reduce.16.cloned.1.call-update) | async-done | bytes 8388624 | tf_op jit(solution)/shard_map/psum | solution.py:200
  1391.7 5.9 fusion.13
  1397.7 22.9 %all-reduce.6 = (bf16[2048]{0:T(1024)(128)(2,1)S(1)}, bf16[2048]{0:T(1024)(128)(2,1)S(1)}) all-reduce(bf16[2048]{0:T(1024)(128)(2,1)S(1)} %get-tuple-element.54, bf16[2048]{0:T(1024)(128)(2,1)S(1)} %copy-done.41), channel_id=2, replica_groups=mesh['dp'=8,'tensor'=4] {'dp'}, use_global_device_ids=true, to_apply=%region_17.18.clone | all-reduce | flops 4096 | bytes 16384
  1421.9 8.6 add_convert_fusion.1
  1430.5 6.9 fusion.18
  1437.4 106.4 %reduce-scatter.20.cloned.1.call-done = bf16[2048,256]{1,0:T(8,128)(2,1)} async-done(((bf16[2048,2048]{1,0:T(8,128)(2,1)}), bf16[2048,256]{1,0:T(8,128)(2,1)}) %reduce-scatter.20.cloned.1.call-update) | async-done | bytes 1048592 | tf_op jit(solution)/shard_map/reduce_scatter | solution.py:275
  1546.5 147.4 %reduce-scatter.18.cloned.1.call-done = bf16[256,2048]{1,0:T(8,128)(2,1)} async-done(((bf16[2048,2048]{1,0:T(8,128)(2,1)}), bf16[256,2048]{1,0:T(8,128)(2,1)}) %reduce-scatter.18.cloned.1.call-update) | async-done | bytes 1048592 | tf_op jit(solution)/shard_map/reduce_scatter | solution.py:272
  1696.7 147.3 %reduce-scatter.16.cloned.1.call-done = bf16[256,2048]{1,0:T(8,128)(2,1)} async-done(((bf16[2048,2048]{1,0:T(8,128)(2,1)}), bf16[256,2048]{1,0:T(8,128)(2,1)}) %reduce-scatter.16.cloned.1.call-update) | async-done | bytes 1048592 | tf_op jit(solution)/shard_map/reduce_scatter | solution.py:269
  (210 shorter events, 73.1 us)
Async XLA Ops:
  7.2 104.9 %all-gather.8.cloned.1.call-start = ((), (), s32[]{:S(2)}) async-start(), calls=%async_computation.7 | async-start | bytes 2359296 | tf_op jit(solution)/shard_map/all_gather | solution.py:161
  7.9 158.7 %all-gather.10.cloned.1.call-start = ((), (), s32[]{:S(2)}) async-start(), calls=%async_computation.8 | async-start | bytes 2359296 | tf_op jit(solution)/shard_map/all_gather | solution.py:164
  8.7 315.8 %all-reduce.12.cloned.1.call-start = ((), (), s32[]{:S(2)}) async-start(), calls=%async_computation.9 | async-start | bytes 16777216 | tf_op jit(solution)/shard_map/psum | solution.py:193
  14.6 96.5 %copy-start.37 = (f32[1024]{0:T(1024)}, f32[1024]{0:T(1024)S(1)}, u32[]{:S(2)}) copy-start(f32[1024]{0:T(1024)S(1)} %fusion.50) | copy-start | bytes 12292
  38.0 73.1 %copy-start.33 = (f32[8,1,256]{2,1,0:T(1,128)}, f32[8,1,256]{2,1,0:T(1,128)S(1)}, u32[]{:S(2)}) copy-start(f32[8,1,256]{2,1,0:T(1,128)S(1)} %convert_element_type.247) | copy-start | bytes 24580
  38.6 65.6 %copy-start.26 = (f32[1,1024,32]{1,2,0:T(8,128)}, f32[1,1024,32]{1,2,0:T(8,128)S(1)}, u32[]{:S(2)}) copy-start(f32[1,1024,32]{1,2,0:T(8,128)S(1)} %get-tuple-element.87) | copy-start | bytes 393220
  38.6 65.6 %copy-start.28 = (f32[1,1024,32]{1,2,0:T(8,128)}, f32[1,1024,32]{1,2,0:T(8,128)S(1)}, u32[]{:S(2)}) copy-start(f32[1,1024,32]{1,2,0:T(8,128)S(1)} %get-tuple-element.88) | copy-start | bytes 393220
  38.6 79.0 %copy-start.24 = (f32[1024,64]{0,1:T(8,128)}, f32[1024,64]{0,1:T(8,128)S(1)}, u32[]{:S(2)}) copy-start(f32[1024,64]{0,1:T(8,128)S(1)} %maximum_bitcast_fusion) | copy-start | bytes 786436
  38.7 78.9 %copy-start.22 = (f32[1024,64]{0,1:T(8,128)}, f32[1024,64]{0,1:T(8,128)S(1)}, u32[]{:S(2)}) copy-start(f32[1024,64]{0,1:T(8,128)S(1)} %maximum_bitcast_fusion.1) | copy-start | bytes 786436
  71.8 39.3 %copy-start.15 = (bf16[2048,128]{1,0:T(8,128)(2,1)}, bf16[2048,128]{1,0:T(8,128)(2,1)S(1)}, u32[]{:S(2)}) copy-start(bf16[2048,128]{1,0:T(8,128)(2,1)S(1)} %all_gather.29) | copy-start | bytes 1572868
  111.9 48.3 %copy-start.8 = (pred[512,1024]{0,1:T(8,128)(4,1)}, pred[512,1024]{0,1:T(8,128)(4,1)S(1)}, u32[]{:S(2)}) copy-start(pred[512,1024]{0,1:T(8,128)(4,1)S(1)} %get-tuple-element.89) | copy-start | bytes 1572868
  112.0 23.2 %copy-start.11 = (bf16[1024,2,64,1]{0,2,3,1:T(8,128)(2,1)}, bf16[1024,2,64,1]{0,2,3,1:T(8,128)(2,1)S(1)}, u32[]{:S(2)}) copy-start(bf16[1024,2,64,1]{0,2,3,1:T(8,128)(2,1)S(1)} %fusion.46) | copy-start | bytes 786436
  118.3 7.8 copy-start.19
  118.3 17.0 copy-start.17
  151.8 8.4 copy-start.31
  151.8 10.7 copy-start
  166.6 7.6 copy-start.47
  174.2 276.9 %all-gather.14.cloned.1.call-start = ((), (), s32[]{:S(2)}) async-start(), calls=%async_computation.11 | async-start | bytes 9437184 | tf_op jit(solution)/shard_map/all_gather | solution.py:167
  174.8 401.0 %all-gather.12.cloned.1.call-start = ((), (), s32[]{:S(2)}) async-start(), calls=%async_computation.10 | async-start | bytes 9437184 | tf_op jit(solution)/shard_map/all_gather | solution.py:166
  175.4 525.4 %all-gather.16.cloned.1.call-start = ((), (), s32[]{:S(2)}) async-start(), calls=%async_computation.12 | async-start | bytes 9437184 | tf_op jit(solution)/shard_map/all_gather | solution.py:168
  176.0 724.6 %all-reduce.14.cloned.1.call-start = ((), (), s32[]{:S(2)}) async-start(), calls=%async_computation.13 | async-start | bytes 16777216 | tf_op jit(solution)/shard_map/psum | solution.py:211
  722.5 13.2 copy-start.51
  749.4 346.3 %reduce-scatter.12.cloned.1.call-start = ((), (), s32[]{:S(2)}) async-start(), calls=%async_computation.16 | async-start | bytes 589824 | tf_op jit(solution)/shard_map/reduce_scatter | solution.py:260
  900.6 7.9 copy-start.21
  908.5 9.6 copy-start.43
  908.5 16.3 slice-start
  908.5 16.3 slice-start.1
  908.5 16.3 slice-start.2
  930.6 9.4 copy-start.9
  940.0 13.8 copy-start.32
  940.0 13.8 copy-start.50
  953.8 8.7 copy-start.5
  953.8 10.9 copy-start.35
  964.6 132.6 %reduce-scatter.10.cloned.1.call-start = ((), (), s32[]{:S(2)}) async-start(), calls=%async_computation.15 | async-start | bytes 589824 | tf_op jit(solution)/shard_map/reduce_scatter | solution.py:257
  964.7 30.0 %copy-start.20 = (bf16[1,512,8,64]{1,3,2,0:T(8,128)(2,1)S(1)}, bf16[1,512,8,64]{1,3,2,0:T(8,128)(2,1)}, u32[]{:S(2)}) copy-start(bf16[1,512,8,64]{1,3,2,0:T(8,128)(2,1)} %copy-done.19) | copy-start | bytes 1572868
  1006.0 159.3 %reduce-scatter.14.cloned.1.call-start = ((), (), s32[]{:S(2)}) async-start(), calls=%async_computation.17 | async-start | bytes 2359296 | tf_op jit(solution)/shard_map/reduce_scatter | solution.py:263
  1013.1 223.7 %reduce-scatter.8.cloned.1.call-start = ((), (), s32[]{:S(2)}) async-start(), calls=%async_computation.14 | async-start | bytes 2359296 | tf_op jit(solution)/shard_map/reduce_scatter | solution.py:254
  1029.5 362.2 %all-reduce.16.cloned.1.call-start = ((), (), s32[]{:S(2)}) async-start(), calls=%async_computation.21 | async-start | bytes 16777216 | tf_op jit(solution)/shard_map/psum | solution.py:200
  1029.6 13.9 copy-start.16
  1050.7 493.1 %reduce-scatter.20.cloned.1.call-start = ((), (), s32[]{:S(2)}) async-start(), calls=%async_computation.20 | async-start | bytes 9437184 | tf_op jit(solution)/shard_map/reduce_scatter | solution.py:275
  1065.2 628.8 %reduce-scatter.18.cloned.1.call-start = ((), (), s32[]{:S(2)}) async-start(), calls=%async_computation.19 | async-start | bytes 9437184 | tf_op jit(solution)/shard_map/reduce_scatter | solution.py:272
  1079.3 764.7 %reduce-scatter.16.cloned.1.call-start = ((), (), s32[]{:S(2)}) async-start(), calls=%async_computation.18 | async-start | bytes 9437184 | tf_op jit(solution)/shard_map/reduce_scatter | solution.py:269
  1093.8 298.0 %copy-start.34 = (f32[8,1,256]{2,1,0:T(1,128)S(1)}, f32[8,1,256]{2,1,0:T(1,128)}, u32[]{:S(2)}) copy-start(f32[8,1,256]{2,1,0:T(1,128)} %copy-done.33) | copy-start | bytes 24580
  1093.8 298.0 %copy-start.38 = (f32[1024]{0:T(1024)S(1)}, f32[1024]{0:T(1024)}, u32[]{:S(2)}) copy-start(f32[1024]{0:T(1024)} %copy-done.37) | copy-start | bytes 12292
  1093.8 303.9 %copy-start.41 = (bf16[2048]{0:T(1024)(128)(2,1)S(1)}, bf16[2048]{0:T(1024)(128)(2,1)}, u32[]{:S(2)}) copy-start(bf16[2048]{0:T(1024)(128)(2,1)} %get-tuple-element.52) | copy-start | bytes 12292
  1093.8 328.1 %copy-start.40 = (f32[1024]{0:T(1024)S(1)}, f32[1024]{0:T(1024)}, u32[]{:S(2)}) copy-start(f32[1024]{0:T(1024)} %copy-done.39) | copy-start | bytes 12292
  1421.9 8.6 copy-start.2
  1421.9 8.6 copy-start.10
  (23 other events, 86.4 us)
Sparse Core Ops, SparseCore 0:
  10.1 57.9 all-gather.7
  70.1 52.7 all-gather.9
  174.3 150.0 all-reduce.11
  326.4 124.6 all-gather.13
  453.1 122.6 all-gather.11
  577.7 123.1 all-gather.15
  749.5 151.0 all-reduce.13
  964.7 62.7 reduce-scatter.11
  1031.5 61.6 reduce-scatter.9
  1097.1 68.1 reduce-scatter.13
  1169.4 67.4 reduce-scatter.7
  1239.8 151.8 all-reduce.15
  1395.4 148.4 reduce-scatter.19
  1547.3 146.5 reduce-scatter.17
  1697.4 146.5 reduce-scatter.15
where the time goes:
time: 1860 us; the launch traced here: 1850 us
  waiting for transfers between devices  1310 us (70%)
  matrix products  262 us (14%)
  blocking collectives  127 us (7%)
  other arithmetic  124 us (7%)
    psum x1, waiting for transfers between devices, shards(): lax.psum(ffn_part.astype(jnp.bfloat16), 'tensor').astype(jnp.float32)  153 us
    psum x1, waiting for transfers between devices, shards(): normed_two_grad = lax.psum(mlp_part, 'tensor')  150 us
    reduce_scatter x1, waiting for transfers between devices, shards(): lax.psum_scatter(up_weight_grad.astype(jnp.bfloat16), 'dp', scatter_dimen...  147 us
    reduce_scatter x1, waiting for transfers between devices, shards(): lax.psum_scatter(gate_weight_grad.astype(jnp.bfloat16), 'dp', scatter_dim...  147 us
    psum x1, waiting for transfers between devices, shards(): hidden_state = tokens_float + lax.psum(attn_part, 'tensor')  132 us
    all_gather x1, waiting for transfers between devices, shards(): lax.all_gather(up_weight, 'dp', axis=0, tiled=True)  115 us
    all_gather x1, waiting for transfers between devices, shards(): lax.all_gather(down_weight, 'dp', axis=1, tiled=True)  110 us
    all_gather x1, waiting for transfers between devices, shards(): lax.all_gather(gate_weight, 'dp', axis=0, tiled=True)  110 us
  transfers between devices with their start and end apart: 15, of which 11 were waited for; matrix products, arithmetic and copies ran while one was open for 14% of the time, Pallas kernels for 0%

commit v1 on v0

--- a/solution.py
+++ b/solution.py
@@ -7,6 +7,22 @@
 
 HD = 64
 epsilon = 1e-05
+
+
+def _replace_links(mat):
+    q_n = jax.lax.axis_size("tensor")
+
+    def show_zones(b_next, finding):
+        if finding >= q_n:
+            return b_next
+        nodes = []
+        w = 0
+        while w < q_n:
+            nodes.append((w, w ^ finding))
+            w = w + 1
+        return show_zones(b_next + jax.lax.ppermute(b_next, "tensor", nodes), 2 * finding)
+
+    return show_zones(mat, 1)
 
 
 def rope_tables(segment_row, head_size):
@@ -208,7 +224,7 @@
     gate_weight_grad = contract_rows(normed_two, gate_low)
     up_weight_grad = contract_rows(normed_two, up_low)
     mlp_part = contract_cols(gate_low, gathered[6]) + contract_cols(up_low, gathered[7])
-    normed_two_grad = lax.psum(mlp_part, "tensor")
+    normed_two_grad = _replace_links(mlp_part)
     unused_second, second_pull = jax.vjp(rms_norm, hidden_state, ffn_scale)
     hidden_part, ffn_gain_grad = second_pull(normed_two_grad)
     hidden_grad = cotangent_float + hidden_part

time: 1860 us -> 1630 us (0.88)
  waiting for transfers between devices: 1310 us -> 1050 us
  other arithmetic: 124 us -> 144 us
    ppermute x0 -> x2, waiting for transfers between devices: none -> 180 us  [show_zones(): jax.lax.ppermute(b_next, 'tensor', nodes)]
    psum x1 -> x0, waiting for transfers between devices: 150 us -> none  [shards(): normed_two_grad = lax.psum(mlp_part, 'tensor')]
    reduce_scatter x1, waiting for transfers between devices: 147 us -> 0.02 us  [shards(): lax.psum_scatter(up_weight_grad.astype(jnp.bfloat16), 'dp', scatter_dimen...]
    reduce_scatter x1, waiting for transfers between devices: 147 us -> 0.01 us  [shards(): lax.psum_scatter(gate_weight_grad.astype(jnp.bfloat16), 'dp', scatter_dim...]
    reduce_scatter x1, waiting for transfers between devices: 106 us -> 23.9 us  [shards(): lax.psum_scatter(down_grad.astype(jnp.bfloat16), 'dp', scatter_dimension=...]
    reduce_scatter x1, waiting for transfers between devices: 0.01 us -> 64.1 us  [shards(): lax.psum_scatter(key_weight_grad.astype(jnp.bfloat16), 'dp', scatter_dime...]
    reduce_scatter x1, waiting for transfers between devices: 0.02 us -> 62.8 us  [shards(): lax.psum_scatter(value_weight_grad.astype(jnp.bfloat16), 'dp', scatter_di...]
    reduce_scatter x1, waiting for transfers between devices: 69.8 us -> 27.2 us  [shards(): lax.psum_scatter(query_weight_grad.astype(jnp.bfloat16), 'dp', scatter_di...]
  transfers between devices with their start and end apart: 15 -> 16, of which waited for: 11 -> 12; matrix products, arithmetic and copies ran while one was open for 14% -> 23% of each run, Pallas kernels for 0% -> 0%
where the time goes in v1:
time: 1630 us; the launch traced here: 1620 us
  waiting for transfers between devices  1050 us (64%)
  matrix products  267 us (16%)
  other arithmetic  144 us (9%)
  blocking collectives  126 us (8%)
    ppermute x2, waiting for transfers between devices, show_zones(): jax.lax.ppermute(b_next, 'tensor', nodes)  180 us
    psum x1, waiting for transfers between devices, shards(): lax.psum(ffn_part.astype(jnp.bfloat16), 'tensor').astype(jnp.float32)  153 us
    psum x1, waiting for transfers between devices, shards(): hidden_state = tokens_float + lax.psum(attn_part, 'tensor')  132 us
    all_gather x1, waiting for transfers between devices, shards(): lax.all_gather(up_weight, 'dp', axis=0, tiled=True)  115 us
    all_gather x1, waiting for transfers between devices, shards(): lax.all_gather(down_weight, 'dp', axis=1, tiled=True)  111 us
    all_gather x1, waiting for transfers between devices, shards(): lax.all_gather(gate_weight, 'dp', axis=0, tiled=True)  110 us
    reduce_scatter x1, waiting for transfers between devices, shards(): lax.psum_scatter(output_weight_grad.astype(jnp.bfloat16), 'dp', scatter_d...  69.8 us
    reduce_scatter x1, waiting for transfers between devices, shards(): lax.psum_scatter(key_weight_grad.astype(jnp.bfloat16), 'dp', scatter_dime...  64.1 us
  transfers between devices with their start and end apart: 16, of which 12 were waited for; matrix products, arithmetic and copies ran while one was open for 23% of the time, Pallas kernels for 0%

profile of v1, /device:TPU:0, one launch (start us, length us, event | category | flops | bytes accessed | tf_op | source)
XLA Modules:
  0.0 1621.4 jit_solution(9338486502861592312)
XLA Ops:
  15.5 22.5 %all-gather = bf16[8,1,256]{2,1,0:T(2,128)(2,1)S(1)} all-gather(bf16[1,1,256]{2,1,0:T(2,128)(2,1)S(1)} %reshape.443), channel_id=1, replica_groups=mesh['dp'=8,'tensor'=4] {'dp'}, dimensions={0}, use_global_device_ids=true | all-gather | bytes 4608 | tf_op jit(solution)/shard_map/all_gather | solution.py:176
  38.7 33.1 %all_gather.29 = bf16[2048,128]{1,0:T(8,128)(2,1)S(1)} all-gather(bf16[256,128]{1,0:T(8,128)(2,1)} %param.16), channel_id=1, replica_groups=mesh['dp'=8,'tensor'=4] {'dp'}, dimensions={0}, use_global_device_ids=true | all-gather | bytes 589824 | tf_op jit(solution)/shard_map/all_gather | solution.py:178
  71.8 32.3 %all_gather.28 = bf16[2048,128]{1,0:T(8,128)(2,1)S(1)} all-gather(bf16[256,128]{1,0:T(8,128)(2,1)} %param.17), channel_id=1, replica_groups=mesh['dp'=8,'tensor'=4] {'dp'}, dimensions={0}, use_global_device_ids=true | all-gather | bytes 589824 | tf_op jit(solution)/shard_map/all_gather | solution.py:179
  118.5 7.8 fusion.11
  126.2 9.2 exponential_reduce_fusion
  135.5 7.3 fusion.10
  142.8 9.2 exponential_reduce_fusion.1
  152.0 8.3 convolution_convert_fusion.8
  166.8 7.5 fusion.41
  176.2 16.3 %all-gather.1 = bf16[8,1,256]{2,1,0:T(2,128)(2,1)S(1)} all-gather(bf16[1,1,256]{2,1,0:T(2,128)(2,1)S(1)} %reshape.445), channel_id=1, replica_groups=mesh['dp'=8,'tensor'=4] {'dp'}, dimensions={0}, use_global_device_ids=true | all-gather | bytes 4608 | tf_op jit(solution)/shard_map/all_gather | solution.py:181
  192.5 132.1 %all-reduce.11.cloned.1.call-done = f32[1024,2048]{1,0:T(8,128)} async-done(((f32[1024,2048]{1,0:T(8,128)}), f32[1024,2048]{1,0:T(8,128)}) %all-reduce.11.cloned.1.call-update) | async-done | bytes 8388624 | tf_op jit(solution)/shard_map/psum | solution.py:209
  324.6 5.7 multiply_reduce_fusion.2
  336.5 114.8 %all-gather.14.cloned.1.call-done = bf16[2048,2048]{1,0:T(8,128)(2,1)} async-done(((bf16[256,2048]{1,0:T(8,128)(2,1)}), bf16[2048,2048]{1,0:T(8,128)(2,1)}) %all-gather.14.cloned.1.call-update) | async-done | bytes 8388624 | tf_op jit(solution)/shard_map/all_gather | solution.py:183
  451.2 14.6 fusion.66
  465.9 110.0 %all-gather.12.cloned.1.call-done = bf16[2048,2048]{1,0:T(8,128)(2,1)} async-done(((bf16[256,2048]{1,0:T(8,128)(2,1)}), bf16[2048,2048]{1,0:T(8,128)(2,1)}) %all-gather.12.cloned.1.call-update) | async-done | bytes 8388624 | tf_op jit(solution)/shard_map/all_gather | solution.py:182
  575.9 14.5 fusion.65
  590.4 110.6 %all-gather.16.cloned.1.call-done = bf16[2048,2048]{1,0:T(8,128)(2,1)} async-done(((bf16[2048,256]{1,0:T(8,128)(2,1)}), bf16[2048,2048]{1,0:T(8,128)(2,1)}) %all-gather.16.cloned.1.call-update) | async-done | bytes 8388624 | tf_op jit(solution)/shard_map/all_gather | solution.py:184
  701.0 21.7 %multiply_convert_fusion = (bf16[1024,2048]{1,0:T(8,128)(2,1)}, bf16[1024,2048]{1,0:T(8,128)(2,1)}, bf16[1024,2048]{1,0:T(8,128)(2,1)}) fusion(f32[1024,2048]{1,0:T(8,128)} %fusion.65, f32[1024,2048]{1,0:T(8,128)} %fusion.66, bf16[1024,2048]{1,0:T(8,128)(2,1)} %param.23, bf16[2048,2048]{1,0:T(8,128)(2,1)} %all-gather.16.cloned.1.call-done), kind=kOutput, calls=%fused_computation.44 | convolution fusion | flops 8623489024 | bytes 41943040 | tf_op jit(solution)/shard_map/dot_general | solution.py:77
  722.6 14.5 convolution_convert_fusion.1
  737.2 14.1 convolution_convert_fusion.2
  751.4 12.8 fusion.67
  764.2 12.7 convolution_add_fusion
  780.3 13.3 collective-permute-done
  793.6 12.0 add.176
  807.1 13.5 convolution_convert_fusion
  821.6 166.7 %collective-permute-done.1 = f32[1024,2048]{1,0:T(8,128)} collective-permute-done((f32[1024,2048]{1,0:T(8,128)}, f32[1024,2048]{1,0:T(8,128)}, u32[]{:S(2)}, u32[]{:S(2)}) %collective-permute-start.1) | collective-permute-done | bytes 8388640 | tf_op jit(solution)/shard_map/ppermute | solution.py:23
  988.3 10.7 multiply_reduce_fusion
  999.1 14.8 fusion.17
  1013.9 7.0 fusion.32
  1026.2 8.4 fusion.40
  1036.8 12.2 fusion.3
  1049.0 11.9 fusion
  1060.9 30.9 %fusion.2 = (bf16[2,4,512,1024]{2,3,1,0:T(8,128)(2,1)}, bf16[2,4,512,1024]{2,3,1,0:T(8,128)(2,1)}) fusion(f32[2,1024,512,4]{2,1,3,0:T(8,128)} %get-tuple-element.98, f32[2,1024,512,4]{2,1,3,0:T(8,128)} %get-tuple-element.94, f32[2,4,512]{2,1,0:T(4,128)S(1)} %get-tuple-element.97, f32[2,4,512]{2,1,0:T(4,128)S(1)} %bitcast.237, ...), kind=kLoop, calls=%fused_computation.4 | loop fusion | flops 50331648 | bytes 85000192 | tf_op jit(solution)/shard_map/while/body/eval_jaxpr/convert_element_type | solution.py:139
  1091.8 6.1 convolution_bitcast_fusion.2
  1098.1 6.2 fusion.38
  1106.9 7.2 convolution_convert_fusion.4
  1114.2 14.0 convolution_convert_fusion.3
  1147.1 5.9 convolution_convert_fusion.5
  1159.9 23.9 %reduce-scatter.20.cloned.1.call-done = bf16[2048,256]{1,0:T(8,128)(2,1)} async-done(((bf16[2048,2048]{1,0:T(8,128)(2,1)}), bf16[2048,256]{1,0:T(8,128)(2,1)}) %reduce-scatter.20.cloned.1.call-update) | async-done | bytes 1048592 | tf_op jit(solution)/shard_map/reduce_scatter | solution.py:291
  1186.5 62.8 %reduce-scatter.12.cloned.1.call-done = bf16[256,128]{1,0:T(8,128)(2,1)} async-done(((bf16[2048,128]{1,0:T(8,128)(2,1)}), bf16[256,128]{1,0:T(8,128)(2,1)}) %reduce-scatter.12.cloned.1.call-update) | async-done | bytes 65552 | tf_op jit(solution)/shard_map/reduce_scatter | solution.py:276
  1250.8 64.1 %reduce-scatter.10.cloned.1.call-done = bf16[256,128]{1,0:T(8,128)(2,1)} async-done(((bf16[2048,128]{1,0:T(8,128)(2,1)}), bf16[256,128]{1,0:T(8,128)(2,1)}) %reduce-scatter.10.cloned.1.call-update) | async-done | bytes 65552 | tf_op jit(solution)/shard_map/reduce_scatter | solution.py:273
  1316.5 69.8 %reduce-scatter.14.cloned.1.call-done = bf16[512,256]{1,0:T(8,128)(2,1)} async-done(((bf16[512,2048]{1,0:T(8,128)(2,1)}), bf16[512,256]{1,0:T(8,128)(2,1)}) %reduce-scatter.14.cloned.1.call-update) | async-done | bytes 262160 | tf_op jit(solution)/shard_map/reduce_scatter | solution.py:279
  1388.1 152.8 %all-reduce.13.cloned.1.call-done = (bf16[1024,2048]{1,0:T(8,128)(2,1)}, bf16[1024,2048]{1,0:T(8,128)(2,1)}) async-done(((bf16[1024,2048]{1,0:T(8,128)(2,1)}, bf16[1024,2048]{1,0:T(8,128)(2,1)}), (bf16[1024,2048]{1,0:T(8,128)(2,1)}, bf16[1024,2048]{1,0:T(8,128)(2,1)})) %all-reduce.13.cloned.1.call-update) | async-done | bytes 8388624 | tf_op jit(solution)/shard_map/psum | solution.py:216
  1540.9 5.9 fusion.13
  1546.8 22.1 %all-reduce.6 = (bf16[2048]{0:T(1024)(128)(2,1)S(1)}, bf16[2048]{0:T(1024)(128)(2,1)S(1)}) all-reduce(bf16[2048]{0:T(1024)(128)(2,1)S(1)} %get-tuple-element.54, bf16[2048]{0:T(1024)(128)(2,1)S(1)} %get-tuple-element.52), channel_id=2, replica_groups=mesh['dp'=8,'tensor'=4] {'dp'}, use_global_device_ids=true, to_apply=%region_16.17.clone | all-reduce | flops 4096 | bytes 16384
  1570.2 8.5 add_convert_fusion.1
  1578.8 6.8 fusion.18
  1585.6 27.2 %reduce-scatter.8.cloned.1.call-done = bf16[256,512]{1,0:T(8,128)(2,1)} async-done(((bf16[2048,512]{1,0:T(8,128)(2,1)}), bf16[256,512]{1,0:T(8,128)(2,1)}) %reduce-scatter.8.cloned.1.call-update) | async-done | bytes 262160 | tf_op jit(solution)/shard_map/reduce_scatter | solution.py:270
  (226 shorter events, 89.1 us)
Async XLA Ops:
  7.2 104.9 %all-gather.8.cloned.1.call-start = ((), (), s32[]{:S(2)}) async-start(), calls=%async_computation.7 | async-start | bytes 2359296 | tf_op jit(solution)/shard_map/all_gather | solution.py:177
  7.9 158.9 %all-gather.10.cloned.1.call-start = ((), (), s32[]{:S(2)}) async-start(), calls=%async_computation.8 | async-start | bytes 2359296 | tf_op jit(solution)/shard_map/all_gather | solution.py:180
  8.7 315.9 %all-reduce.11.cloned.1.call-start = ((), (), s32[]{:S(2)}) async-start(), calls=%async_computation.9 | async-start | bytes 16777216 | tf_op jit(solution)/shard_map/psum | solution.py:209
  14.6 96.5 %copy-start.46 = (f32[1024]{0:T(1024)}, f32[1024]{0:T(1024)S(1)}, u32[]{:S(2)}) copy-start(f32[1024]{0:T(1024)S(1)} %fusion.50) | copy-start | bytes 12292
  38.0 73.1 %copy-start.39 = (f32[8,1,256]{2,1,0:T(1,128)}, f32[8,1,256]{2,1,0:T(1,128)S(1)}, u32[]{:S(2)}) copy-start(f32[8,1,256]{2,1,0:T(1,128)S(1)} %convert_element_type.247) | copy-start | bytes 24580
  38.6 65.6 %copy-start.29 = (f32[1,1024,32]{1,2,0:T(8,128)}, f32[1,1024,32]{1,2,0:T(8,128)S(1)}, u32[]{:S(2)}) copy-start(f32[1,1024,32]{1,2,0:T(8,128)S(1)} %get-tuple-element.87) | copy-start | bytes 393220
  38.6 65.6 %copy-start.31 = (f32[1,1024,32]{1,2,0:T(8,128)}, f32[1,1024,32]{1,2,0:T(8,128)S(1)}, u32[]{:S(2)}) copy-start(f32[1,1024,32]{1,2,0:T(8,128)S(1)} %get-tuple-element.88) | copy-start | bytes 393220
  38.6 79.1 %copy-start.25 = (f32[1024,64]{0,1:T(8,128)}, f32[1024,64]{0,1:T(8,128)S(1)}, u32[]{:S(2)}) copy-start(f32[1024,64]{0,1:T(8,128)S(1)} %maximum_bitcast_fusion) | copy-start | bytes 786436
  38.7 79.1 %copy-start.23 = (f32[1024,64]{0,1:T(8,128)}, f32[1024,64]{0,1:T(8,128)S(1)}, u32[]{:S(2)}) copy-start(f32[1024,64]{0,1:T(8,128)S(1)} %maximum_bitcast_fusion.1) | copy-start | bytes 786436
  71.8 39.3 %copy-start.16 = (bf16[2048,128]{1,0:T(8,128)(2,1)}, bf16[2048,128]{1,0:T(8,128)(2,1)S(1)}, u32[]{:S(2)}) copy-start(bf16[2048,128]{1,0:T(8,128)(2,1)S(1)} %all_gather.29) | copy-start | bytes 1572868
  109.6 50.7 %copy-start.27 = (bf16[1024,128]{0,1:T(8,128)(2,1)}, bf16[1024,128]{0,1:T(8,128)(2,1)S(1)}, u32[]{:S(2)}) copy-start(bf16[1024,128]{0,1:T(8,128)(2,1)S(1)} %convolution_convert_fusion.10) | copy-start | bytes 786436
  111.9 40.1 %copy-start.8 = (pred[512,1024]{0,1:T(8,128)(4,1)}, pred[512,1024]{0,1:T(8,128)(4,1)S(1)}, u32[]{:S(2)}) copy-start(pred[512,1024]{0,1:T(8,128)(4,1)S(1)} %get-tuple-element.90) | copy-start | bytes 1572868
  111.9 48.4 %copy-start.6 = (pred[512,1024]{0,1:T(8,128)(4,1)}, pred[512,1024]{0,1:T(8,128)(4,1)S(1)}, u32[]{:S(2)}) copy-start(pred[512,1024]{0,1:T(8,128)(4,1)S(1)} %get-tuple-element.89) | copy-start | bytes 1572868
  112.1 23.4 %copy-start.12 = (bf16[1024,2,64,1]{0,2,3,1:T(8,128)(2,1)}, bf16[1024,2,64,1]{0,2,3,1:T(8,128)(2,1)S(1)}, u32[]{:S(2)}) copy-start(bf16[1024,2,64,1]{0,2,3,1:T(8,128)(2,1)S(1)} %fusion.46) | copy-start | bytes 786436
  118.5 17.0 %copy-start.18 = (bf16[1,512,8,64]{1,3,2,0:T(8,128)(2,1)}, bf16[1,512,8,64]{1,3,2,0:T(8,128)(2,1)S(1)}, u32[]{:S(2)}) copy-start(bf16[1,512,8,64]{1,3,2,0:T(8,128)(2,1)S(1)} %get-tuple-element.81) | copy-start | bytes 1572868
  135.4 16.5 %copy-start.35 = (f32[1,8,512]{2,1,0:T(8,128)}, f32[1,8,512]{2,1,0:T(8,128)S(1)}, u32[]{:S(2)}) copy-start(f32[1,8,512]{2,1,0:T(8,128)S(1)} %log_add_fusion) | copy-start | bytes 49156
  152.0 10.7 copy-start
  174.4 276.9 %all-gather.14.cloned.1.call-start = ((), (), s32[]{:S(2)}) async-start(), calls=%async_computation.11 | async-start | bytes 9437184 | tf_op jit(solution)/shard_map/all_gather | solution.py:183
  175.0 400.9 %all-gather.12.cloned.1.call-start = ((), (), s32[]{:S(2)}) async-start(), calls=%async_computation.10 | async-start | bytes 9437184 | tf_op jit(solution)/shard_map/all_gather | solution.py:182
  175.5 525.4 %all-gather.16.cloned.1.call-start = ((), (), s32[]{:S(2)}) async-start(), calls=%async_computation.12 | async-start | bytes 9437184 | tf_op jit(solution)/shard_map/all_gather | solution.py:184
  176.1 978.2 %reduce-scatter.18.cloned.1.call-start = ((), (), s32[]{:S(2)}) async-start(), calls=%async_computation.18 | async-start | bytes 9437184 | tf_op jit(solution)/shard_map/reduce_scatter | solution.py:288
  192.5 138.4 %copy-start.41 = (f32[8,1,256]{2,1,0:T(1,128)}, f32[8,1,256]{2,1,0:T(1,128)S(1)}, u32[]{:S(2)}) copy-start(f32[8,1,256]{2,1,0:T(1,128)S(1)} %convert_element_type.248) | copy-start | bytes 24580
  737.1 420.0 %reduce-scatter.16.cloned.1.call-start = ((), (), s32[]{:S(2)}) async-start(), calls=%async_computation.17 | async-start | bytes 9437184 | tf_op jit(solution)/shard_map/reduce_scatter | solution.py:285
  751.3 432.4 %reduce-scatter.20.cloned.1.call-start = ((), (), s32[]{:S(2)}) async-start(), calls=%async_computation.19 | async-start | bytes 9437184 | tf_op jit(solution)/shard_map/reduce_scatter | solution.py:291
  780.3 26.8 %copy-start.22 = (bf16[1024,2048]{1,0:T(8,128)(2,1)S(1)}, bf16[1024,2048]{1,0:T(8,128)(2,1)}, u32[]{:S(2)}) copy-start(bf16[1024,2048]{1,0:T(8,128)(2,1)} %param.23) | copy-start | bytes 12582916
  780.3 13.3 collective-permute-start
  805.6 182.8 %collective-permute-start.1 = (f32[1024,2048]{1,0:T(8,128)}, f32[1024,2048]{1,0:T(8,128)}, u32[]{:S(2)}, u32[]{:S(2)}) collective-permute-start(f32[1024,2048]{1,0:T(8,128)} %add.176), channel_id=1, source_target_pairs={{0,2},{1,3},{2,0},{3,1},{4,6},{5,7},{6,4},{7,5},{8,10},{9,11},{10,... | collective-permute-start | bytes 25165832 | tf_op jit(solution)/shard_map/ppermute | solution.py:23
  820.5 167.8 %copy-start.42 = (f32[8,1,256]{2,1,0:T(1,128)S(1)}, f32[8,1,256]{2,1,0:T(1,128)}, u32[]{:S(2)}) copy-start(f32[8,1,256]{2,1,0:T(1,128)} %copy-done.41) | copy-start | bytes 24580
  820.5 167.8 %copy-start.44 = (f32[1024]{0:T(1024)S(1)}, f32[1024]{0:T(1024)}, u32[]{:S(2)}) copy-start(f32[1024]{0:T(1024)} %copy-done.43) | copy-start | bytes 12292
  820.6 428.7 %reduce-scatter.12.cloned.1.call-start = ((), (), s32[]{:S(2)}) async-start(), calls=%async_computation.15 | async-start | bytes 589824 | tf_op jit(solution)/shard_map/reduce_scatter | solution.py:276
  821.6 177.5 %copy-start.51 = (f32[1024]{0:T(1024)S(1)}, f32[1024]{0:T(1024)}, u32[]{:S(2)}) copy-start(f32[1024]{0:T(1024)} %copy-done.50) | copy-start | bytes 12292
  999.1 21.9 %slice-start = ((s8[16777216]{0:T(1024)(128)(4,1)}), s8[4194304]{0:T(1024)(128)(4,1)S(1)}, s32[]{:S(2)}) async-start(s8[16777216]{0:T(1024)(128)(4,1)} %bitcast.210), calls=%async_computation.21 | async-start | bytes 8388608
  999.1 21.9 %slice-start.1 = ((s8[16777216]{0:T(1024)(128)(4,1)}), s8[4194304]{0:T(1024)(128)(4,1)S(1)}, s32[]{:S(2)}) async-start(s8[16777216]{0:T(1024)(128)(4,1)} %bitcast.210), calls=%async_computation.22 | async-start | bytes 8388608
  999.1 21.9 %slice-start.2 = ((s8[16777216]{0:T(1024)(128)(4,1)}), s8[4194304]{0:T(1024)(128)(4,1)S(1)}, s32[]{:S(2)}) async-start(s8[16777216]{0:T(1024)(128)(4,1)} %bitcast.210), calls=%async_computation.23 | async-start | bytes 8388608
  1026.2 10.6 copy-start.28
  1026.2 10.6 copy-start.38
  1034.7 14.3 copy-start.33
  1060.9 30.9 %copy-start.21 = (bf16[1,512,8,64]{1,3,2,0:T(8,128)(2,1)S(1)}, bf16[1,512,8,64]{1,3,2,0:T(8,128)(2,1)}, u32[]{:S(2)}) copy-start(bf16[1,512,8,64]{1,3,2,0:T(8,128)(2,1)} %copy-done.20) | copy-start | bytes 1572868
  1098.0 217.0 %reduce-scatter.10.cloned.1.call-start = ((), (), s32[]{:S(2)}) async-start(), calls=%async_computation.14 | async-start | bytes 589824 | tf_op jit(solution)/shard_map/reduce_scatter | solution.py:273
  1098.0 8.9 copy-start.55
  1098.0 8.9 copy-start.57
  1106.7 279.6 %reduce-scatter.14.cloned.1.call-start = ((), (), s32[]{:S(2)}) async-start(), calls=%async_computation.16 | async-start | bytes 2359296 | tf_op jit(solution)/shard_map/reduce_scatter | solution.py:279
  1114.1 14.1 copy-start.13
  1114.1 426.8 %all-reduce.13.cloned.1.call-start = ((), (), s32[]{:S(2)}) async-start(), calls=%async_computation.20 | async-start | bytes 16777216 | tf_op jit(solution)/shard_map/psum | solution.py:216
  1146.8 466.0 %reduce-scatter.8.cloned.1.call-start = ((), (), s32[]{:S(2)}) async-start(), calls=%async_computation.13 | async-start | bytes 2359296 | tf_op jit(solution)/shard_map/reduce_scatter | solution.py:270
  1153.0 387.9 %copy-start.40 = (f32[8,1,256]{2,1,0:T(1,128)S(1)}, f32[8,1,256]{2,1,0:T(1,128)}, u32[]{:S(2)}) copy-start(f32[8,1,256]{2,1,0:T(1,128)} %copy-done.39) | copy-start | bytes 24580
  1153.0 387.9 %copy-start.47 = (f32[1024]{0:T(1024)S(1)}, f32[1024]{0:T(1024)}, u32[]{:S(2)}) copy-start(f32[1024]{0:T(1024)} %copy-done.46) | copy-start | bytes 12292
  1157.1 413.1 %copy-start.49 = (f32[1024]{0:T(1024)S(1)}, f32[1024]{0:T(1024)}, u32[]{:S(2)}) copy-start(f32[1024]{0:T(1024)} %copy-done.48) | copy-start | bytes 12292
  (31 other events, 146.4 us)
Sparse Core Ops, SparseCore 0:
  10.1 57.9 all-gather.7
  70.1 52.7 all-gather.9
  174.5 150.0 all-reduce.10
  326.6 124.6 all-gather.13
  453.2 122.6 all-gather.11
  577.8 123.1 all-gather.15
  737.3 145.6 reduce-scatter.17
  886.5 146.5 reduce-scatter.15
  1036.8 146.9 reduce-scatter.19
  1187.5 61.7 reduce-scatter.11
  1253.2 61.6 reduce-scatter.9
  1318.3 67.9 reduce-scatter.13
  1388.9 151.9 all-reduce.12
  1544.3 68.4 reduce-scatter.7
